TPU v7x, 128 devices: a whole 4x4x4 slice. The times are simulated.
128 devices in a mesh: rows: 32 (over x, z, core), units: 4 (over y).
Axes of the slice: x: 4, y: 4, z: 4, core: 2. Of those that a mesh axis runs over, the one named last changes fastest.
Arguments:
- residuals: bfloat16 [524288, 2048], P(('rows', 'units')), may hold values from -24 to 24
- loadings: bfloat16 [524288, 256], P(('rows', 'units')), may hold values from -6 to 6
- zero_points: bfloat16 [1024, 2048], P('units'), may hold values from -0.375 to 0.375
- sketch_matrix: bfloat16 [2048, 256], replicated, may hold values from -0.125 to 0.125
- use_lists: int32 [4096, 4], P(('rows', 'units')), may hold values from 0 to 15, all different within a row
Outputs:
- star_basis: float32 [524288, 256], P(('rows', 'units'))
- bin_modes: float32 [2048, 256], P(('rows', 'units'))
Inputs may be any that keep to these rules, and one draw needn't show every extreme that they name: `use_lists`: each row names 4 different groups; every group is named by some row.
All inputs are finite; a program needn't handle non-finite values.
Results may differ from a plain program's by a relative error of at most 0.003.
Values may be sent and summed in bfloat16 or wider, within the bound.
No kernel may reach another device: no remote copies, remote signals or barrier semaphores. Data moves between devices by JAX's collectives and lax.ppermute only.
A program may use at most 192 MiB of HBM per device.

v0:
```python
import jax
import jax.numpy as jnp
from jax import lax
from jax.sharding import PartitionSpec as P

GROUP = 64
USES = 4
BLOCK_STARS = 128


def on_device(residuals, loadings, zero_points, sketch_matrix, use_lists):
    gathered = lax.all_gather(zero_points, "units", axis=0, tiled=True)
    local_rows, width_bins = residuals.shape
    group_count = gathered.shape[0] // GROUP
    block_count = use_lists.shape[0]
    tables = gathered.reshape(group_count, GROUP, width_bins)
    chosen = tables[use_lists].reshape(block_count, USES * GROUP, width_bins)
    offsets = jnp.einsum(
        "bsk,bkn->bsn",
        loadings.reshape(block_count, BLOCK_STARS, USES * GROUP),
        chosen,
        preferred_element_type=jnp.float32,
    )
    corrected = (
        residuals.reshape(block_count, BLOCK_STARS, width_bins).astype(jnp.float32) - offsets
    ).astype(jnp.bfloat16)
    corrected = corrected.reshape(local_rows, width_bins)
    sketched = jnp.dot(corrected, sketch_matrix, preferred_element_type=jnp.float32)
    sketch_low = sketched.astype(jnp.bfloat16)
    devices_all = lax.axis_size(("rows", "units"))
    total_stars = local_rows * devices_all
    gram_local = jnp.dot(sketched.T, sketched, precision=lax.Precision.HIGHEST) / total_stars
    lower_factor = jnp.linalg.cholesky(lax.psum(gram_local, ("rows", "units")))
    star_basis = lax.linalg.triangular_solve(
        lower_factor, sketched, left_side=False, lower=True, transpose_a=True
    )
    bin_share = width_bins // devices_all
    full_terms = jnp.einsum("sn,sm->nm", corrected, sketch_low, preferred_element_type=jnp.float32)
    summed_all = lax.psum(full_terms, ("rows", "units"))
    first_bin = lax.axis_index(("rows", "units")) * bin_share
    summed = lax.dynamic_slice_in_dim(summed_all, first_bin, bin_share, 0)
    raw_modes = summed / total_stars
    bin_modes = lax.linalg.triangular_solve(
        lower_factor, raw_modes, left_side=False, lower=True, transpose_a=True
    )
    return (star_basis, bin_modes)


def solution(mesh):
    in_specs = (
        P(("rows", "units"), None),
        P(("rows", "units"), None),
        P("units", None),
        P(),
        P(("rows", "units"), None),
    )
    out_specs = (P(("rows", "units"), None), P(("rows", "units"), None))
    return jax.shard_map(
        on_device, mesh=mesh, in_specs=in_specs, out_specs=out_specs, check_vma=False
    )
```

profile of v0, /device:TPU:1, one launch (start us, length us, event | category | flops | bytes accessed | tf_op | source)
XLA Modules:
  0.0 364.4 jit_solution(14588423251606039512)
XLA Ops:
  7.2 0.0 copy-start
  7.2 0.0 all-gather.2.cloned.1.call-start
  7.2 0.7 all-gather.2.cloned.1.call-update
  7.9 0.0 all-reduce.4.cloned.1.call-start
  8.0 0.7 compare_select_fusion
  8.6 0.1 copy.11
  8.7 0.1 reshape.66
  8.9 52.1 %all-gather.2.cloned.1.call-done = bf16[1024,2048]{1,0:T(8,128)(2,1)} async-done(((bf16[256,2048]{1,0:T(8,128)(2,1)}), bf16[1024,2048]{1,0:T(8,128)(2,1)}) %all-gather.2.cloned.1.call-update) | async-done | bytes 4194320 | tf_op jit(solution)/shard_map/all_gather | solution.py:12
  60.9 14.9 %gather_fusion = bf16[128,64,2048]{2,1,0:T(8,128)(2,1)} fusion(bf16[16,64,2048]{2,1,0:T(8,128)(2,1)} %bitcast.51, s32[1024]{0:T(1024)S(1)} %pad_clamp_fusion), kind=kCustom, calls=%fused_computation | custom fusion | bytes 67109376 | tf_op jit(solution)/shard_map/gather | solution.py:17
  75.8 0.0 copy-done
  75.8 23.4 %fusion = bf16[32,128,2048]{2,1,0:T(8,128)(2,1)} fusion(bf16[32,128,2048]{2,1,0:T(8,128)(2,1)} %bitcast.53, bf16[32,128,256]{2,1,0:T(8,128)(2,1)S(1)} %bitcast.50, bf16[32,256,2048]{2,1,0:T(8,128)(2,1)} %bitcast.52), kind=kOutput, calls=%fused_computation.4 | convolution fusion | flops 4320133120 | bytes 69206016 | tf_op jit(solution)/shard_map/bsk,bkn->bsn/dot_general | solution.py:18
  99.2 0.0 copy-done.5
  99.3 10.3 %fusion.16 = f32[4096,256]{1,0:T(8,128)S(1)} fusion(bf16[4096,2048]{1,0:T(8,128)(2,1)} %bitcast.54, bf16[2048,256]{1,0:T(8,128)(2,1)S(1)} %copy-done.5), kind=kOutput, calls=%fused_computation.44 | convolution fusion | flops 4294967296 | bytes 22020096 | tf_op jit(solution)/shard_map/dot_general | solution.py:28
  109.6 0.2 copy-done.4
  109.8 6.3 %fusion.3 = f32[2048,256]{1,0:T(8,128)} fusion(bf16[4096,2048]{1,0:T(8,128)(2,1)S(1)} %bitcast.55, f32[4096,256]{1,0:T(8,128)S(1)} %fusion.16), kind=kOutput, calls=%fused_computation.9 | convolution fusion | flops 4296015872 | bytes 23068672 | tf_op jit(solution)/shard_map/sn,sm->nm/dot_general | solution.py:38
  116.1 0.0 copy-done.2
  116.1 7.4 %convolution_multiply_fusion = f32[256,256]{0,1:T(8,128)} fusion(f32[4096,256]{1,0:T(8,128)S(1)} %fusion.16), kind=kOutput, calls=%fused_computation.11 | convolution fusion | flops 3221291008 | bytes 4456448 | tf_op jit(solution)/shard_map/dot_general | solution.py:32
  123.6 0.0 all-reduce.4.cloned.1.call-update
  123.6 152.5 %all-reduce.4.cloned.1.call-done = (f32[256,256]{0,1:T(8,128)}, f32[2048,256]{1,0:T(8,128)}) async-done(((f32[256,256]{0,1:T(8,128)}, f32[2048,256]{1,0:T(8,128)}), (f32[256,256]{0,1:T(8,128)}, f32[2048,256]{1,0:T(8,128)})) %all-reduce.4.cloned.1.call-update) | async-done | bytes 2359312 | tf_op jit(solution)/shard_map/psum | solution.py:33
  276.1 1.2 copy.13
  277.4 1.0 fusion.5
  278.4 11.7 %cholesky.50 = f32[128,128]{1,0:T(8,128)S(1)} custom-call(f32[128,128]{1,0:T(8,128)S(1)} %cholesky.118), custom_call_target="Cholesky" | custom-call | tf_op jit(solution)/shard_map/jit(cholesky)/cholesky | solution.py:33
  290.1 9.8 %custom-call.16 = f32[1,128,128]{1,2,0:T(8,128)S(1)} custom-call(f32[1,128,128]{2,1,0:T(8,128)S(1)} %get-tuple-element.29), custom_call_target="InvertDiagBlocksLowerTriangular" | custom-call | tf_op jit(solution)/shard_map/jit(cholesky)/cholesky | solution.py:33
  300.0 0.2 constant_dynamic-update-slice_fusion.1
  300.2 0.3 convolution_subtract_fusion.1
  300.5 11.7 %cholesky.105 = f32[128,128]{1,0:T(8,128)S(1)} custom-call(f32[128,128]{1,0:T(8,128)S(1)} %convolution_subtract_fusion.1), custom_call_target="Cholesky" | custom-call | tf_op jit(solution)/shard_map/jit(cholesky)/cholesky | solution.py:33
  312.2 0.7 compare_reduce_fusion
  314.2 0.1 triangular_solve.73
  314.3 3.9 %while.1 = (s32[]{:T(128)}, f32[256,256]{1,0:T(8,128)S(1)}, s32[2,2]{1,0:T(2,128)S(1)}, f32[2,128,128]{2,1,0:T(8,128)S(1)}, s32[]{:T(128)}) while((s32[]{:T(128)}, f32[256,256]{1,0:T(8,128)S(1)}, s32[2,2]{1,0:T(2,128)S(1)}, f32[2,128,128]{2,1,0:T(8,128)S(1)}, s32[]{:T(128)}) %tuple.29), condition=%wide.while_cond, body=%wide.while_body.sunk | while | flops 2 | bytes 131181 | solution.py:34
  314.3 0.6 fusion.31
  314.9 1.3 bitcast_dynamic-update-slice_fusion.2
  316.2 0.6 fusion.31
  316.8 1.3 bitcast_dynamic-update-slice_fusion.2
  318.1 19.9 %custom-call.17 = f32[2,128,128]{1,2,0:T(8,128)S(1)} custom-call(f32[2,128,128]{2,1,0:T(8,128)S(1)} %get-tuple-element.9), custom_call_target="InvertDiagBlocksLowerTriangular" | custom-call | tf_op jit(solution)/shard_map/triangular_solve | solution.py:34
  338.0 0.0 copy-start.3
  338.1 3.7 %fusion.1 = f32[4096,128]{0,1:T(8,128)S(1)} fusion(f32[4096,256]{1,0:T(8,128)} %copy-done.2, f32[2,128,128]{1,2,0:T(8,128)S(1)} %custom-call.17), kind=kOutput, calls=%fused_computation.7 | convolution fusion | flops 805306368 | bytes 4259840 | tf_op jit(solution)/shard_map/triangular_solve | solution.py:34
  341.8 0.7 dynamic-slice_multiply_fusion
  342.5 0.2 fusion.9
  342.7 0.2 convolution_subtract_fusion.2
  342.9 0.2 fusion.10
  343.1 0.6 pad_maximum_fusion.1
  343.7 0.0 copy-done.3
  343.7 3.6 convolution_subtract_fusion
  347.3 2.0 fusion.11
  349.3 0.0 copy-start.1
  349.3 2.4 pad_maximum_fusion
  351.7 5.6 %copy.14 = f32[4096,256]{1,0:T(8,128)} copy(f32[4096,256]{0,1:T(8,128)} %pad_maximum_fusion) | data formatting | bytes 8388608
  357.3 0.0 copy-done.1
  (13 shorter events, 0.2 us)
Async XLA Ops:
  7.2 68.7 %copy-start = (bf16[4096,256]{1,0:T(8,128)(2,1)S(1)}, bf16[4096,256]{1,0:T(8,128)(2,1)}, u32[]{:S(2)}) copy-start(bf16[4096,256]{1,0:T(8,128)(2,1)} %param.6) | copy-start | bytes 6291460
  7.2 53.8 %all-gather.2.cloned.1.call-start = ((), (), s32[]{:S(2)}) async-start(), calls=%async_computation | async-start | bytes 5242880 | tf_op jit(solution)/shard_map/all_gather | solution.py:12
  7.9 268.2 %all-reduce.4.cloned.1.call-start = ((), (), s32[]{:S(2)}) async-start(), calls=%async_computation.1 | async-start | bytes 4718592 | tf_op jit(solution)/shard_map/psum | solution.py:33
  75.8 23.4 %copy-start.5 = (bf16[2048,256]{1,0:T(8,128)(2,1)S(1)}, bf16[2048,256]{1,0:T(8,128)(2,1)}, u32[]{:S(2)}) copy-start(bf16[2048,256]{1,0:T(8,128)(2,1)} %param.8) | copy-start | bytes 3145732
  99.3 10.5 %copy-start.4 = (bf16[32,128,2048]{2,1,0:T(8,128)(2,1)S(1)}, bf16[32,128,2048]{2,1,0:T(8,128)(2,1)}, u32[]{:S(2)}) copy-start(bf16[32,128,2048]{2,1,0:T(8,128)(2,1)} %fusion) | copy-start | bytes 50331652
  109.8 6.3 %copy-start.2 = (f32[4096,256]{1,0:T(8,128)}, f32[4096,256]{1,0:T(8,128)S(1)}, u32[]{:S(2)}) copy-start(f32[4096,256]{1,0:T(8,128)S(1)} %fusion.16) | copy-start | bytes 12582916
  338.0 5.7 %copy-start.3 = (f32[4096,256]{1,0:T(8,128)S(1)}, f32[4096,256]{1,0:T(8,128)}, u32[]{:S(2)}) copy-start(f32[4096,256]{1,0:T(8,128)} %copy-done.2) | copy-start | bytes 12582916
  349.3 8.0 %copy-start.1 = (bf16[4096,256]{1,0:T(8,128)(2,1)S(1)}, bf16[4096,256]{1,0:T(8,128)(2,1)}, u32[]{:S(2)}) copy-start(bf16[4096,256]{1,0:T(8,128)(2,1)} %param.6) | copy-start | bytes 6291460
Sparse Core Ops, SparseCore 0:
  9.7 51.2 all-gather.1
  123.7 152.3 all-reduce.3
where the time goes:
time: 369 us; the launch traced here: 364 us
  waiting for transfers between devices  205 us (56%)
  other arithmetic  59.4 us (16%)
  matrix products  57.9 us (16%)
  local copies, waits for them, and re-layouts  26.1 us (7%)
  between operations  15.7 us (4%)
    psum x1, waiting for transfers between devices, on_device(): lower_factor = jnp.linalg.cholesky(lax.psum(gram_local, ('rows', 'units')))  153 us
    all_gather x1, waiting for transfers between devices, on_device(): gathered = lax.all_gather(zero_points, 'units', axis=0, tiled=True)  52.1 us
    another operation x6, other arithmetic, on_device(): lower_factor = jnp.linalg.cholesky(lax.psum(gram_local, ('rows', 'units')))  34 us
    dot_general x1, matrix products, on_device(): jnp.einsum('bsk,bkn->bsn', loadings.reshape(block_count, BLOCK_STARS, USE...  23.4 us
    another operation x4, other arithmetic, on_device(): lax.linalg.triangular_solve(lower_factor, sketched, left_side=False, lowe...  22.3 us
    gather x1, local copies, waits for them, and re-layouts, on_device(): chosen = tables[use_lists].reshape(block_count, USES * GROUP, width_bins)  14.9 us
    dot_general x1, matrix products, on_device(): jnp.dot(corrected, sketch_matrix, preferred_element_type=jnp.float32)  10.3 us
    another operation x3, matrix products, on_device(): lax.linalg.triangular_solve(lower_factor, sketched, left_side=False, lowe...  9.32 us
  transfers between devices with their start and end apart: 2, of which 2 were waited for; matrix products, arithmetic and copies ran while one was open for 0% of the time, Pallas kernels for 0%

commit v1 on v0

--- a/solution.py
+++ b/solution.py
@@ -1,3 +1,4 @@
+import functools
 import jax
 import jax.numpy as jnp
 from jax import lax
@@ -6,6 +7,15 @@
 GROUP = 64
 USES = 4
 BLOCK_STARS = 128
+
+
+def switch_thing(inputs, dev_axis, along_axis):
+    k_now = lax.psum(inputs, axis_name=dev_axis)
+    inter = lax.psum(k_now, axis_name=along_axis)
+    return inter
+
+
+sources_all_arrange = functools.partial(switch_thing, dev_axis="rows", along_axis="units")
 
 
 def on_device(residuals, loadings, zero_points, sketch_matrix, use_lists):
@@ -30,7 +40,7 @@
     devices_all = lax.axis_size(("rows", "units"))
     total_stars = local_rows * devices_all
     gram_local = jnp.dot(sketched.T, sketched, precision=lax.Precision.HIGHEST) / total_stars
-    lower_factor = jnp.linalg.cholesky(lax.psum(gram_local, ("rows", "units")))
+    lower_factor = jnp.linalg.cholesky(sources_all_arrange(gram_local))
     star_basis = lax.linalg.triangular_solve(
         lower_factor, sketched, left_side=False, lower=True, transpose_a=True
     )

time: 369 us -> 438 us (1.19)
  waiting for transfers between devices: 205 us -> 263 us
  matrix products: 57.9 us -> 63.1 us
    psum x1 -> x3, waiting for transfers between devices: 153 us -> 211 us  [the longest x1 103 us: switch_thing(): k_now = lax.psum(inputs, axis_name=dev_axis)]
    dot_general x1, matrix products: 6.31 us -> 13.2 us  [on_device(): jnp.einsum('sn,sm->nm', corrected, sketch_low, preferred_element_type=jnp...]
  transfers between devices with their start and end apart: 2 -> 4, of which waited for: 2 -> 4; matrix products, arithmetic and copies ran while one was open for 0% -> 21% of each run, Pallas kernels for 0% -> 0%
where the time goes in v1:
time: 438 us; the launch traced here: 430 us
  waiting for transfers between devices  263 us (60%)
  matrix products  63.1 us (14%)
  other arithmetic  59.4 us (14%)
  local copies, waits for them, and re-layouts  27.9 us (6%)
  between operations  15.6 us (4%)
    psum x1, waiting for transfers between devices, switch_thing(): k_now = lax.psum(inputs, axis_name=dev_axis)  103 us
    psum x1, waiting for transfers between devices, on_device(): summed_all = lax.psum(full_terms, ('rows', 'units'))  79.4 us
    all_gather x1, waiting for transfers between devices, on_device(): gathered = lax.all_gather(zero_points, 'units', axis=0, tiled=True)  52.1 us
    another operation x6, other arithmetic, on_device(): lower_factor = jnp.linalg.cholesky(sources_all_arrange(gram_local))  34.2 us
    psum x1, waiting for transfers between devices, switch_thing(): inter = lax.psum(k_now, axis_name=along_axis)  28.1 us
    dot_general x1, matrix products, on_device(): jnp.einsum('bsk,bkn->bsn', loadings.reshape(block_count, BLOCK_STARS, USE...  23.4 us
    another operation x4, other arithmetic, on_device(): lax.linalg.triangular_solve(lower_factor, sketched, left_side=False, lowe...  22.1 us
    gather x1, local copies, waits for them, and re-layouts, on_device(): chosen = tables[use_lists].reshape(block_count, USES * GROUP, width_bins)  14.9 us
  transfers between devices with their start and end apart: 4, of which 4 were waited for; matrix products, arithmetic and copies ran while one was open for 21% of the time, Pallas kernels for 0%

profile of v1, /device:TPU:1, one launch (start us, length us, event | category | flops | bytes accessed | tf_op | source)
XLA Modules:
  0.0 429.6 jit_solution(16348853287514028164)
XLA Ops:
  7.2 0.0 copy-start
  7.2 0.0 all-gather.2.cloned.1.call-start
  7.2 0.7 all-gather.2.cloned.1.call-update
  7.9 0.0 all-reduce.5.cloned.1.call-start
  8.0 0.7 compare_select_fusion
  8.6 0.1 copy.11
  8.7 0.1 reshape.66
  8.9 52.1 %all-gather.2.cloned.1.call-done = bf16[1024,2048]{1,0:T(8,128)(2,1)} async-done(((bf16[256,2048]{1,0:T(8,128)(2,1)}), bf16[1024,2048]{1,0:T(8,128)(2,1)}) %all-gather.2.cloned.1.call-update) | async-done | bytes 4194320 | tf_op jit(solution)/shard_map/all_gather | solution.py:22
  60.9 14.9 %gather_fusion = bf16[128,64,2048]{2,1,0:T(8,128)(2,1)} fusion(bf16[16,64,2048]{2,1,0:T(8,128)(2,1)} %bitcast.51, s32[1024]{0:T(1024)S(1)} %pad_clamp_fusion), kind=kCustom, calls=%fused_computation | custom fusion | bytes 67109376 | tf_op jit(solution)/shard_map/gather | solution.py:27
  75.8 23.4 %fusion = bf16[32,128,2048]{2,1,0:T(8,128)(2,1)} fusion(bf16[32,128,2048]{2,1,0:T(8,128)(2,1)} %bitcast.53, bf16[32,128,256]{2,1,0:T(8,128)(2,1)S(1)} %bitcast.50, bf16[32,256,2048]{2,1,0:T(8,128)(2,1)} %bitcast.52), kind=kOutput, calls=%fused_computation.4 | convolution fusion | flops 4320133120 | bytes 69206016 | tf_op jit(solution)/shard_map/bsk,bkn->bsn/dot_general | solution.py:28
  99.3 8.4 %fusion.16 = f32[4096,256]{1,0:T(8,128)S(1)} fusion(bf16[4096,2048]{1,0:T(8,128)(2,1)} %bitcast.54, bf16[2048,256]{1,0:T(8,128)(2,1)S(1)} %copy-done.4), kind=kOutput, calls=%fused_computation.44 | convolution fusion | flops 4294967296 | bytes 22020096 | tf_op jit(solution)/shard_map/dot_general | solution.py:38
  107.7 2.0 copy-done.2
  109.7 7.6 %convolution_multiply_fusion = f32[256,256]{0,1:T(8,128)} fusion(f32[4096,256]{1,0:T(8,128)S(1)} %fusion.16), kind=kOutput, calls=%fused_computation.11 | convolution fusion | flops 3221291008 | bytes 4456448 | tf_op jit(solution)/shard_map/dot_general | solution.py:42
  117.4 0.0 all-reduce.5.cloned.1.call-update
  117.4 0.0 all-reduce.7.cloned.1.call-start
  117.5 103.1 %all-reduce.5.cloned.1.call-done = f32[256,256]{0,1:T(8,128)} async-done(((f32[256,256]{0,1:T(8,128)}), f32[256,256]{0,1:T(8,128)}) %all-reduce.5.cloned.1.call-update) | async-done | bytes 262160 | tf_op jit(solution)/shard_map/psum | solution.py:13
  220.5 0.0 all-reduce.7.cloned.1.call-update
  220.5 0.2 all-reduce.9.cloned.1.call-start
  220.8 13.2 %fusion.3 = f32[2048,256]{1,0:T(8,128)} fusion(bf16[4096,2048]{1,0:T(8,128)(2,1)} %bitcast.55, f32[4096,256]{1,0:T(8,128)} %copy-done.2), kind=kOutput, calls=%fused_computation.9 | convolution fusion | flops 4296015872 | bytes 23068672 | tf_op jit(solution)/shard_map/sn,sm->nm/dot_general | solution.py:48
  234.0 0.0 all-reduce.9.cloned.1.call-update
  234.0 28.1 %all-reduce.7.cloned.1.call-done = f32[256,256]{0,1:T(8,128)} async-done(((f32[256,256]{0,1:T(8,128)}), f32[256,256]{0,1:T(8,128)}) %all-reduce.7.cloned.1.call-update) | async-done | bytes 262160 | tf_op jit(solution)/shard_map/psum | solution.py:14
  262.1 1.1 copy.13
  263.2 1.0 fusion.5
  264.2 11.7 %cholesky.50 = f32[128,128]{1,0:T(8,128)S(1)} custom-call(f32[128,128]{1,0:T(8,128)S(1)} %cholesky.118), custom_call_target="Cholesky" | custom-call | tf_op jit(solution)/shard_map/jit(cholesky)/cholesky | solution.py:43
  275.9 9.8 %custom-call.16 = f32[1,128,128]{1,2,0:T(8,128)S(1)} custom-call(f32[1,128,128]{2,1,0:T(8,128)S(1)} %get-tuple-element.27), custom_call_target="InvertDiagBlocksLowerTriangular" | custom-call | tf_op jit(solution)/shard_map/jit(cholesky)/cholesky | solution.py:43
  285.8 0.2 constant_dynamic-update-slice_fusion.1
  286.0 0.3 convolution_subtract_fusion.1
  286.2 11.9 %cholesky.105 = f32[128,128]{1,0:T(8,128)S(1)} custom-call(f32[128,128]{1,0:T(8,128)S(1)} %convolution_subtract_fusion.1), custom_call_target="Cholesky" | custom-call | tf_op jit(solution)/shard_map/jit(cholesky)/cholesky | solution.py:43
  298.2 0.7 compare_reduce_fusion
  300.2 0.1 triangular_solve.73
  300.3 4.0 while.1
  300.3 0.6 fusion.31
  300.9 1.3 bitcast_dynamic-update-slice_fusion.2
  302.3 0.6 fusion.31
  302.9 1.3 bitcast_dynamic-update-slice_fusion.2
  304.3 19.7 %custom-call.17 = f32[2,128,128]{1,2,0:T(8,128)S(1)} custom-call(f32[2,128,128]{2,1,0:T(8,128)S(1)} %get-tuple-element.9), custom_call_target="InvertDiagBlocksLowerTriangular" | custom-call | tf_op jit(solution)/shard_map/triangular_solve | solution.py:44
  324.0 0.0 copy-start.3
  324.0 3.7 fusion.1
  327.7 3.6 convolution_subtract_fusion
  331.3 2.0 fusion.11
  333.3 2.4 pad_maximum_fusion
  335.7 5.6 %copy.14 = f32[4096,256]{1,0:T(8,128)} copy(f32[4096,256]{0,1:T(8,128)} %pad_maximum_fusion) | data formatting | bytes 8388608
  341.3 79.4 %all-reduce.9.cloned.1.call-done = f32[2048,256]{1,0:T(8,128)} async-done(((f32[2048,256]{1,0:T(8,128)}), f32[2048,256]{1,0:T(8,128)}) %all-reduce.9.cloned.1.call-update) | async-done | bytes 2097168 | tf_op jit(solution)/shard_map/psum | solution.py:49
  420.8 0.7 dynamic-slice_multiply_fusion
  421.5 0.2 fusion.9
  421.7 0.2 convolution_subtract_fusion.2
  421.9 0.2 fusion.10
  422.1 0.6 pad_maximum_fusion.1
  (17 shorter events, 0.2 us)
Async XLA Ops:
  7.2 68.7 %copy-start = (bf16[4096,256]{1,0:T(8,128)(2,1)S(1)}, bf16[4096,256]{1,0:T(8,128)(2,1)}, u32[]{:S(2)}) copy-start(bf16[4096,256]{1,0:T(8,128)(2,1)} %param.6) | copy-start | bytes 6291460
  7.2 53.8 %all-gather.2.cloned.1.call-start = ((), (), s32[]{:S(2)}) async-start(), calls=%async_computation | async-start | bytes 5242880 | tf_op jit(solution)/shard_map/all_gather | solution.py:22
  7.9 212.6 %all-reduce.5.cloned.1.call-start = ((), (), s32[]{:S(2)}) async-start(), calls=%async_computation.1 | async-start | bytes 524288 | tf_op jit(solution)/shard_map/psum | solution.py:13
  75.8 23.4 %copy-start.4 = (bf16[2048,256]{1,0:T(8,128)(2,1)S(1)}, bf16[2048,256]{1,0:T(8,128)(2,1)}, u32[]{:S(2)}) copy-start(bf16[2048,256]{1,0:T(8,128)(2,1)} %param.8) | copy-start | bytes 3145732
  107.7 2.0 copy-start.2
  117.4 144.7 %all-reduce.7.cloned.1.call-start = ((), (), s32[]{:S(2)}) async-start(), calls=%async_computation.2 | async-start | bytes 524288 | tf_op jit(solution)/shard_map/psum | solution.py:14
  220.5 200.2 %all-reduce.9.cloned.1.call-start = ((), (), s32[]{:S(2)}) async-start(), calls=%async_computation.3 | async-start | bytes 4194304 | tf_op jit(solution)/shard_map/psum | solution.py:49
  324.0 3.8 copy-start.3
  333.3 89.4 %copy-start.1 = (bf16[4096,256]{1,0:T(8,128)(2,1)S(1)}, bf16[4096,256]{1,0:T(8,128)(2,1)}, u32[]{:S(2)}) copy-start(bf16[4096,256]{1,0:T(8,128)(2,1)} %param.6) | copy-start | bytes 6291460
Sparse Core Ops, SparseCore 0:
  9.7 51.2 all-gather.1
  117.5 102.9 all-reduce.4
  222.9 39.1 all-reduce.6
  266.8 153.9 all-reduce.8
